TPU v7x, 512 devices: a whole 4x4x16 slice. The times are simulated.
512 devices in a mesh: row: 32 (over x, y, core), col: 16 (over z).
Axes of the slice: x: 4, y: 4, z: 16, core: 2. Of those that a mesh axis runs over, the one named last changes fastest.
Arguments:
- similarity: float32 [8192, 8192], P('row', 'col'), may hold values from 0.1 to 500
- pattern: int32 [32, 32], P('row', 'col'), may hold values from 0 to 1, as said below
Outputs:
- clustered: float32 [8192, 8192], P('row', 'col')
Inputs may be any that keep to these rules, and one draw needn't show every extreme that they name: `pattern`: every diagonal tile (g, g) is stored.
All inputs are finite; a program needn't handle non-finite values.
Results may differ from a plain program's by a relative error of at most 0.0003.
Values may be sent and summed in bfloat16 or wider, within the bound.
A program may use at most 64 MiB of HBM per device.

v0:
```python
import jax
import jax.numpy as jnp
from jax import lax
from jax.sharding import PartitionSpec as P

TILE = 256


def spread(pattern):
    rows, cols = pattern.shape
    values = pattern.astype(jnp.float32)
    return jnp.broadcast_to(values[:, None, :, None], (rows, TILE, cols, TILE)).reshape(
        rows * TILE, cols * TILE
    )


def tile_sum(left_part, right_part):
    return jnp.dot(left_part, right_part, preferred_element_type=jnp.float32)


def product(operand):
    left = lax.all_gather(operand, "col", axis=1, tiled=True)
    return tile_sum(left, lax.all_gather(operand, "row", axis=0, tiled=True))


def shards(similarity, pattern):
    cells = spread(pattern)
    total_rows = similarity.shape[0] * lax.axis_size("row")
    held = similarity * cells
    start_total = lax.psum(jnp.sum(held, axis=0), "row")
    matrix = held * (total_rows / start_total)[None, :]
    operand = matrix.astype(jnp.bfloat16)
    expanded = product(operand) * cells
    inflated = expanded * expanded
    sums = lax.psum(jnp.sum(inflated, axis=0), "row")
    matrix = inflated * (total_rows / sums)[None, :]
    return matrix


def solution(mesh):
    placed = (P("row", "col"), P("row", "col"))
    return jax.shard_map(
        shards, mesh=mesh, in_specs=placed, out_specs=P("row", "col"), check_vma=False
    )
```

profile of v0, /device:TPU:1, one launch (start us, length us, event | category | flops | bytes accessed | tf_op | source)
XLA Modules:
  0.0 302.0 jit_solution(1512720498870579981)
XLA Ops:
  6.5 0.0 all-gather.3.cloned.1.call-start
  6.5 0.7 convert_bitcast_fusion
  7.2 0.1 broadcast_bitcast_fusion
  7.3 1.1 multiply_reduce_fusion
  8.4 68.9 %psum.14 = f32[512]{0:T(512)S(1)} all-reduce(f32[512]{0:T(512)S(1)} %multiply_reduce_fusion), channel_id=1, replica_groups=mesh['row'=32,'col'=16] {'row'}, use_global_device_ids=true, to_apply=%region_1.0 | all-reduce | flops 512 | bytes 4096 | tf_op jit(solution)/shard_map/psum | solution.py:30
  77.3 1.8 multiply_convert_fusion
  79.1 0.0 all-gather.3.cloned.1.call-update
  79.1 0.0 all-gather.5.cloned.1.call-start
  79.2 0.7 all-gather.5.cloned.1.call-update
  79.9 68.0 %all-gather.3.cloned.1.call-done = bf16[256,8192]{1,0:T(8,128)(2,1)} async-done(((bf16[256,512]{1,0:T(8,128)(2,1)}), bf16[256,8192]{1,0:T(8,128)(2,1)}) %all-gather.3.cloned.1.call-update) | async-done | bytes 4194320 | tf_op jit(solution)/shard_map/all_gather | solution.py:22
  147.8 77.2 %all-gather.5.cloned.1.call-done = bf16[8192,512]{1,0:T(8,128)(2,1)} async-done(((bf16[256,512]{1,0:T(8,128)(2,1)}), bf16[8192,512]{1,0:T(8,128)(2,1)}) %all-gather.5.cloned.1.call-update) | async-done | bytes 8388624 | tf_op jit(solution)/shard_map/all_gather | solution.py:23
  225.0 7.0 %fusion.1 = (f32[512]{0:T(512)S(1)}, f32[256,512]{1,0:T(8,128)S(1)}) fusion(f32[512]{0:T(512)S(1)} %bitcast.9, bf16[256,8192]{1,0:T(8,128)(2,1)} %all-gather.3.cloned.1.call-done, bf16[8192,512]{1,0:T(8,128)(2,1)} %all-gather.5.cloned.1.call-done), kind=kOutput, calls=%fused_computation.9 | convolution fusion | flops 2147876352 | bytes 13111296 | tf_op jit(solution)/shard_map/dot_general | solution.py:18
  232.0 62.3 %psum.15 = f32[512]{0:T(512)S(1)} all-reduce(f32[512]{0:T(512)S(1)} %get-tuple-element.5), channel_id=1, replica_groups=mesh['row'=32,'col'=16] {'row'}, use_global_device_ids=true, to_apply=%region_3.0 | all-reduce | flops 512 | bytes 4096 | tf_op jit(solution)/shard_map/psum | solution.py:35
  294.3 0.9 broadcast_multiply_fusion
  (3 shorter events, 0.0 us)
Async XLA Ops:
  6.5 141.3 %all-gather.3.cloned.1.call-start = ((), (), s32[]{:S(2)}) async-start(), calls=%async_computation | async-start | bytes 4456448 | tf_op jit(solution)/shard_map/all_gather | solution.py:22
  79.1 145.9 %all-gather.5.cloned.1.call-start = ((), (), s32[]{:S(2)}) async-start(), calls=%async_computation.1 | async-start | bytes 8650752 | tf_op jit(solution)/shard_map/all_gather | solution.py:23
Sparse Core Ops, SparseCore 0:
  79.2 68.5 all-gather.2
  151.0 73.9 all-gather.4
where the time goes:
time: 304 us; the launch traced here: 302 us
  waiting for transfers between devices  146 us (48%)
  blocking collectives  131 us (43%)
  between operations  13.4 us (4%)
  matrix products  7 us (2%)
  other arithmetic  4.45 us (1%)
    all_gather x1, waiting for transfers between devices, product(): return tile_sum(left, lax.all_gather(operand, 'row', axis=0, tiled=True))  77.2 us
    psum x1, blocking collectives, shards(): start_total = lax.psum(jnp.sum(held, axis=0), 'row')  68.9 us
    all_gather x1, waiting for transfers between devices, product(): left = lax.all_gather(operand, 'col', axis=1, tiled=True)  68 us
    psum x1, blocking collectives, shards(): sums = lax.psum(jnp.sum(inflated, axis=0), 'row')  62.3 us
    dot_general x1, matrix products, tile_sum(): return jnp.dot(left_part, right_part, preferred_element_type=jnp.float32)  7 us
  transfers between devices with their start and end apart: 2, of which 2 were waited for; matrix products, arithmetic and copies ran while one was open for 0% of the time, Pallas kernels for 0%

commit v1 on v0

v1 whole, which is shorter than its diff:
```python
import jax
import jax.numpy as jnp
from jax import lax
from jax.experimental import pallas as pl
from jax.experimental.pallas import tpu as pltpu
from jax.sharding import PartitionSpec as P

MESH = pl.DeviceIdType.MESH
TILE = 256
NX, NY, NZ = 4, 4, 16
HALF = TILE // 2

F_OFF = (0, -1, 1, -2)
FORWARD = (1, -1, 1, -1)


def kernel(
    sim_hbm, pat_ref, out_ref,
    sim, left, right, acc, p1, p2, p3, p4,
    in_sem, z_send, z_recv, f_send, f_recv, s_send, s_recv, d_send, d_recv,
    p_send, p_recv,
):
    row = lax.axis_index("row")
    z = lax.axis_index("col")
    core = lax.rem(row, 2)
    chip = row // 2
    y = lax.rem(chip, NY)
    x = chip // NY
    total_rows = float(NX * NY * 2 * TILE)

    load = pltpu.make_async_copy(sim_hbm, sim, in_sem)
    load.start()

    def row_of(xx, yy, cc):
        return (xx * NY + yy) * 2 + cc

    def at(df, ds, cc):
        dx = df * (1 - cc) + ds * cc
        dy = df * cc + ds * (1 - cc)
        return row_of(lax.rem(x + dx + NX, NX), lax.rem(y + dy + NY, NY), cc)

    x_peers = [
        row_of(lax.rem(x + dx, NX), y, lax.rem(core + dc, 2))
        for dx in range(NX) for dc in range(2) if dx or dc
    ]
    y_peers = [row_of(x, lax.rem(y + dy, NY), core) for dy in range(1, NY)]
    z_next = lax.rem(z + 1, NZ)
    z_prev = lax.rem(z + NZ - 1, NZ)
    sibling = row_of(x, y, 1 - core)

    barrier = pltpu.get_barrier_semaphore()
    for peer in x_peers + y_peers:
        pl.semaphore_signal(barrier, inc=1, device_id=(peer, z), device_id_type=MESH)
    for peer in (z_next, z_prev):
        pl.semaphore_signal(barrier, inc=1, device_id=(row, peer), device_id_type=MESH)
    p_left = pat_ref[0, 0].astype(jnp.float32)
    p_right = pat_ref[0, 1].astype(jnp.float32)
    load.wait()
    sim[:, :TILE] = sim[:, :TILE] * p_left
    sim[:, TILE:] = sim[:, TILE:] * p_right
    part = jnp.sum(sim[...], axis=0, keepdims=True)
    pl.semaphore_wait(barrier, len(x_peers) + len(y_peers) + 2)

    pending = []

    def send(src, dst, send_sem, recv_sem, to):
        copy = pltpu.make_async_remote_copy(
            src_ref=src, dst_ref=dst, send_sem=send_sem, recv_sem=recv_sem,
            device_id=to, device_id_type=MESH,
        )
        copy.start()
        pending.append(copy)
        return copy

    def plane_sum(value, first, second, base):
        slot = x * 2 + core
        first[slot] = value
        copies = [
            send(first.at[slot], first.at[slot], p_send.at[base + i], p_recv.at[base + i], (peer, z))
            for i, peer in enumerate(x_peers)
        ]
        for copy in copies:
            copy.wait_recv()
        second[y] = jnp.sum(first[...], axis=0)
        copies = [
            send(second.at[y], second.at[y], p_send.at[base + 7 + i], p_recv.at[base + 7 + i], (peer, z))
            for i, peer in enumerate(y_peers)
        ]
        for copy in copies:
            copy.wait_recv()
        return jnp.sum(second[...], axis=0)

    total = plane_sum(part, p1, p2, 0)
    operand = (sim[...] * (total_rows / total)).astype(jnp.bfloat16)
    left[z] = operand

    def block(r):
        return right.at[r // 2, pl.ds(lax.rem(r, 2) * TILE, TILE)]

    right[chip, pl.ds(core * TILE, TILE)] = operand

    z_copies = {}

    def z_hop(way, j):
        origin = lax.rem(z - way * (j // 2) + NZ, NZ)
        half = j % 2 if way > 0 else 1 - j % 2
        ref = left.at[origin, pl.ds(half * HALF, HALF)]
        w = 0 if way > 0 else 1
        z_copies[way, j] = send(ref, ref, z_send.at[w, j], z_recv.at[w, j], (row, z_next if way > 0 else z_prev))

    plane = {}

    def plane_hop(df, ds, sems, to_f, to_s, key):
        ref = block(at(df, ds, core))
        plane[key] = send(ref, ref, sems[0], sems[1], (at(to_f, to_s, core), z))

    def f_hop(i, df, way):
        plane_hop(df, 0, (f_send.at[i], f_recv.at[i]), way, 0, ("f", i))

    def s_hop(g, i, ds, way):
        plane_hop(F_OFF[g], ds, (s_send.at[g, i], s_recv.at[g, i]), 0, way, ("s", g, i))

    to_sibling = []

    def share(df, ds):
        i = len(to_sibling)
        ref = block(at(df, ds, core))
        to_sibling.append(send(ref, ref, d_send.at[i], d_recv.at[i], (sibling, z)))

    def spread(g):
        s_hop(g, 0, 0, 1)
        s_hop(g, 1, 0, -1)

    def arrive(key):
        plane[key].wait_recv()
        if key[0] == "f":
            i = key[1]
            if i == 0:
                f_hop(2, -1, 1)
                share(-1, 0)
                spread(1)
            elif i == 1:
                share(1, 0)
                spread(2)
            else:
                share(-2, 0)
                spread(3)
        else:
            _, g, i = key
            way = FORWARD[g]
            if i == 2:
                share(F_OFF[g], -2 * way)
                return
            ds = -1 if i == 0 else 1
            if ds == -way:
                s_hop(g, 2, ds, way)
            share(F_OFF[g], ds)

    z_hop(1, 0)
    z_hop(-1, 0)
    f_hop(0, 0, 1)
    f_hop(1, 0, -1)
    spread(0)
    z_hop(1, 1)
    z_hop(-1, 1)
    share(0, 0)

    def products(first, count):
        def body(i, carry):
            k = lax.rem(z + first + NZ + i, NZ)
            acc[...] += jnp.dot(left[k], right[k], preferred_element_type=jnp.float32)
            return carry
        lax.fori_loop(0, count, body, 0)

    acc[...] = jnp.zeros_like(acc)

    after = {
        1: [("f", 0), ("f", 1), ("s", 0, 0), ("s", 0, 1)],
        3: [("s", 1, 1)],
        4: [("f", 2), ("s", 0, 2), ("s", 2, 1)],
        5: [("s", 1, 0), ("s", 1, 2)],
        6: [("s", 3, 1), ("s", 2, 0)],
        7: [("s", 3, 0), ("s", 3, 2)],
        8: [("s", 2, 2)],
    }
    compute = {
        10: [(-1, 3)],
        11: [(2, 2), (-3, 2)],
        12: [(4, 2), (-5, 2)],
        13: [(6, 2), (-7, 2)],
        14: [(8, 1)],
    }
    last = NZ - 2
    for j in range(last + 1):
        for way in (1, -1):
            z_copies[way, j].wait_recv()
            if j + 2 <= last:
                z_hop(way, j + 2)
        for key in after.get(j, ()):
            arrive(key)
        if j == 9:
            for copy in to_sibling:
                copy.wait_recv()
        for first, count in compute.get(j, ()):
            products(first, count)

    left_part = acc[:, :TILE] * p_left
    right_part = acc[:, TILE:] * p_right
    acc[:, :TILE] = left_part * left_part
    acc[:, TILE:] = right_part * right_part
    sums = plane_sum(jnp.sum(acc[...], axis=0, keepdims=True), p3, p4, 10)
    out_ref[...] = acc[...] * (total_rows / sums)

    for copy in pending:
        copy.wait_send()


def shards(similarity, pattern):
    rows, columns = similarity.shape
    dma = pltpu.SemaphoreType.DMA
    return pl.pallas_call(
        kernel,
        out_shape=jax.ShapeDtypeStruct((rows, columns), jnp.float32),
        in_specs=[
            pl.BlockSpec(memory_space=pl.ANY),
            pl.BlockSpec(memory_space=pltpu.SMEM),
        ],
        out_specs=pl.BlockSpec(memory_space=pltpu.VMEM),
        scratch_shapes=[
            pltpu.VMEM((rows, columns), jnp.float32),
            pltpu.VMEM((NZ, rows, columns), jnp.bfloat16),
            pltpu.VMEM((NX * NY, 2 * rows, columns), jnp.bfloat16),
            pltpu.VMEM((rows, columns), jnp.float32),
            pltpu.VMEM((8, 1, columns), jnp.float32),
            pltpu.VMEM((4, 1, columns), jnp.float32),
            pltpu.VMEM((8, 1, columns), jnp.float32),
            pltpu.VMEM((4, 1, columns), jnp.float32),
            dma, dma((2, NZ - 1)), dma((2, NZ - 1)), dma((3,)), dma((3,)),
            dma((4, 3)), dma((4, 3)), dma((NX * NY,)), dma((NX * NY,)),
            dma((20,)), dma((20,)),
        ],
        compiler_params=pltpu.CompilerParams(collective_id=0, has_side_effects=True),
    )(similarity, pattern)


def solution(mesh):
    placed = (P("row", "col"), P("row", "col"))
    return jax.shard_map(
        shards, mesh=mesh, in_specs=placed, out_specs=P("row", "col"), check_vma=False
    )
```

time: 304 us -> 76.4 us (0.25)
  waiting for transfers between devices: 146 us -> 0 us
  blocking collectives: 131 us -> 0 us
  Pallas kernels: 0 us -> 74.3 us
  between operations: 13.4 us -> 0.01 us
  matrix products: 7 us -> 0 us
  other arithmetic: 4.45 us -> 0 us
    all_gather x2 -> x0, waiting for transfers between devices: 145 us -> none  [the longest x1 77.2 us: product(): return tile_sum(left, lax.all_gather(operand, 'row', axis=0, tiled=True))]
    psum x2 -> x0, blocking collectives: 131 us -> none  [the longest x1 68.9 us: shards(): start_total = lax.psum(jnp.sum(held, axis=0), 'row')]
    pallas_call x0 -> x1, Pallas kernels: none -> 74.3 us  [shards(): pl.pallas_call(kernel, out_shape=jax.ShapeDtypeStruct((rows, columns), jn...]
    dot_general x1 -> x0, matrix products: 7 us -> none  [tile_sum(): return jnp.dot(left_part, right_part, preferred_element_type=jnp.float32)]
  transfers between devices with their start and end apart: 2 -> 0, of which waited for: 2 -> 0; matrix products, arithmetic and copies ran while one was open for 0% -> 0% of each run, Pallas kernels for 0% -> 0%
where the time goes in v1:
time: 76.4 us; the launch traced here: 76.1 us
  Pallas kernels  74.3 us (97%)
  local copies, waits for them, and re-layouts  1.87 us (2%)
    pallas_call x1, Pallas kernels, shards(): pl.pallas_call(kernel, out_shape=jax.ShapeDtypeStruct((rows, columns), jn...  74.3 us
    unnamed x1, local copies, waits for them, and re-layouts  1.87 us

profile of v1, /device:TPU:1, one launch (start us, length us, event | category | flops | bytes accessed | tf_op | source)
XLA Modules:
  0.0 76.1 jit_solution(3147026194654484868)
XLA Ops:
  0.0 74.3 %shard_map.28 = f32[256,512]{1,0:T(8,128)} custom-call(f32[256,512]{1,0:T(8,128)} %sim_hbm.1, s32[1,2]{1,0:T(1,128)} %pat_ref.1), custom_call_target="tpu_custom_call" | custom-call | tf_op jit(solution)/shard_map/pallas_call | solution.py:221
  74.3 1.9 %copy.4 = f32[256,512]{1,0:T(8,128)} copy(f32[256,512]{1,0:T(8,128)} %shard_map.28) | data formatting | bytes 1048576

commit v2 on v1

--- a/solution.py
+++ b/solution.py
@@ -15,8 +15,8 @@
 
 
 def kernel(
-    sim_hbm, pat_ref, out_ref,
-    sim, left, right, acc, p1, p2, p3, p4,
+    sim_hbm, pat_ref, acc, scale_ref,
+    sim, left, right, p1, p2,
     in_sem, z_send, z_recv, f_send, f_recv, s_send, s_recv, d_send, d_recv,
     p_send, p_recv,
 ):
@@ -39,17 +39,16 @@
         dy = df * cc + ds * (1 - cc)
         return row_of(lax.rem(x + dx + NX, NX), lax.rem(y + dy + NY, NY), cc)
 
-    x_peers = [
-        row_of(lax.rem(x + dx, NX), y, lax.rem(core + dc, 2))
-        for dx in range(NX) for dc in range(2) if dx or dc
+    peers = [
+        row_of(lax.rem(x + dx, NX), lax.rem(y + dy, NY), lax.rem(core + dc, 2))
+        for dx in (2, 1, 3, 0) for dy in (2, 1, 3, 0) for dc in (0, 1) if dx or dy or dc
     ]
-    y_peers = [row_of(x, lax.rem(y + dy, NY), core) for dy in range(1, NY)]
     z_next = lax.rem(z + 1, NZ)
     z_prev = lax.rem(z + NZ - 1, NZ)
     sibling = row_of(x, y, 1 - core)
 
     barrier = pltpu.get_barrier_semaphore()
-    for peer in x_peers + y_peers:
+    for peer in peers:
         pl.semaphore_signal(barrier, inc=1, device_id=(peer, z), device_id_type=MESH)
     for peer in (z_next, z_prev):
         pl.semaphore_signal(barrier, inc=1, device_id=(row, peer), device_id_type=MESH)
@@ -59,7 +58,7 @@
     sim[:, :TILE] = sim[:, :TILE] * p_left
     sim[:, TILE:] = sim[:, TILE:] * p_right
     part = jnp.sum(sim[...], axis=0, keepdims=True)
-    pl.semaphore_wait(barrier, len(x_peers) + len(y_peers) + 2)
+    pl.semaphore_wait(barrier, len(peers) + 2)
 
     pending = []
 
@@ -72,25 +71,17 @@
         pending.append(copy)
         return copy
 
-    def plane_sum(value, first, second, base):
-        slot = x * 2 + core
-        first[slot] = value
+    def plane_sum(value, parts, base):
+        parts[row] = value
         copies = [
-            send(first.at[slot], first.at[slot], p_send.at[base + i], p_recv.at[base + i], (peer, z))
-            for i, peer in enumerate(x_peers)
+            send(parts.at[row], parts.at[row], p_send.at[base + i], p_recv.at[base + i], (peer, z))
+            for i, peer in enumerate(peers)
         ]
         for copy in copies:
             copy.wait_recv()
-        second[y] = jnp.sum(first[...], axis=0)
-        copies = [
-            send(second.at[y], second.at[y], p_send.at[base + 7 + i], p_recv.at[base + 7 + i], (peer, z))
-            for i, peer in enumerate(y_peers)
-        ]
-        for copy in copies:
-            copy.wait_recv()
-        return jnp.sum(second[...], axis=0)
-
-    total = plane_sum(part, p1, p2, 0)
+        return jnp.sum(parts[...], axis=0)
+
+    total = plane_sum(part, p1, 0)
     operand = (sim[...] * (total_rows / total)).astype(jnp.bfloat16)
     left[z] = operand
 
@@ -208,8 +199,8 @@
     right_part = acc[:, TILE:] * p_right
     acc[:, :TILE] = left_part * left_part
     acc[:, TILE:] = right_part * right_part
-    sums = plane_sum(jnp.sum(acc[...], axis=0, keepdims=True), p3, p4, 10)
-    out_ref[...] = acc[...] * (total_rows / sums)
+    sums = plane_sum(jnp.sum(acc[...], axis=0, keepdims=True), p2, len(peers))
+    scale_ref[...] = total_rows / sums
 
     for copy in pending:
         copy.wait_send()
@@ -218,29 +209,31 @@
 def shards(similarity, pattern):
     rows, columns = similarity.shape
     dma = pltpu.SemaphoreType.DMA
-    return pl.pallas_call(
+    planes = NX * NY * 2
+    inflated, scale = pl.pallas_call(
         kernel,
-        out_shape=jax.ShapeDtypeStruct((rows, columns), jnp.float32),
+        out_shape=(
+            pltpu.VMEM((rows, columns), jnp.float32),
+            pltpu.VMEM((1, columns), jnp.float32),
+        ),
         in_specs=[
             pl.BlockSpec(memory_space=pl.ANY),
             pl.BlockSpec(memory_space=pltpu.SMEM),
         ],
-        out_specs=pl.BlockSpec(memory_space=pltpu.VMEM),
+        out_specs=(pl.BlockSpec(memory_space=pltpu.VMEM),) * 2,
         scratch_shapes=[
             pltpu.VMEM((rows, columns), jnp.float32),
             pltpu.VMEM((NZ, rows, columns), jnp.bfloat16),
             pltpu.VMEM((NX * NY, 2 * rows, columns), jnp.bfloat16),
-            pltpu.VMEM((rows, columns), jnp.float32),
-            pltpu.VMEM((8, 1, columns), jnp.float32),
-            pltpu.VMEM((4, 1, columns), jnp.float32),
-            pltpu.VMEM((8, 1, columns), jnp.float32),
-            pltpu.VMEM((4, 1, columns), jnp.float32),
+            pltpu.VMEM((planes, 1, columns), jnp.float32),
+            pltpu.VMEM((planes, 1, columns), jnp.float32),
             dma, dma((2, NZ - 1)), dma((2, NZ - 1)), dma((3,)), dma((3,)),
             dma((4, 3)), dma((4, 3)), dma((NX * NY,)), dma((NX * NY,)),
-            dma((20,)), dma((20,)),
+            dma((2 * planes - 2,)), dma((2 * planes - 2,)),
         ],
         compiler_params=pltpu.CompilerParams(collective_id=0, has_side_effects=True),
     )(similarity, pattern)
+    return inflated * scale
 
 
 def solution(mesh):

time: 76.4 us -> 74.2 us (0.971)
  local copies, waits for them, and re-layouts: 1.87 us -> 0 us
  Pallas kernels: 74.3 us -> 73.1 us
  other arithmetic: 0 us -> 0.86 us
    unnamed x1 -> x0, local copies, waits for them, and re-layouts: 1.87 us -> none
    pallas_call x1, Pallas kernels: 74.3 us -> 73.1 us  [shards(): pl.pallas_call(kernel, out_shape=(pltpu.VMEM((rows, columns), jnp.float32...]
    mul x0 -> x1, other arithmetic: none -> 0.86 us  [shards(): return inflated * scale]
where the time goes in v2:
time: 74.2 us; the launch traced here: 74 us
  Pallas kernels  73.1 us (99%)
  other arithmetic  0.86 us (1%)
    pallas_call x1, Pallas kernels, shards(): pl.pallas_call(kernel, out_shape=(pltpu.VMEM((rows, columns), jnp.float32...  73.1 us

profile of v2, /device:TPU:1, one launch (start us, length us, event | category | flops | bytes accessed | tf_op | source)
XLA Modules:
  0.0 74.0 jit_solution(4651155526158391499)
XLA Ops:
  0.0 73.1 %shard_map.28 = (f32[256,512]{1,0:T(8,128)S(1)}, f32[1,512]{1,0:T(1,128)S(1)}) custom-call(f32[256,512]{1,0:T(8,128)} %sim_hbm.1, s32[1,2]{1,0:T(1,128)} %pat_ref.1), custom_call_target="tpu_custom_call" | custom-call | tf_op jit(solution)/shard_map/pallas_call | solution.py:213
  73.1 0.9 %broadcast_multiply_fusion = f32[256,512]{1,0:T(8,128)} fusion(f32[256,512]{1,0:T(8,128)S(1)} %get-tuple-element.7, f32[512]{0:T(512)S(1)} %bitcast.1), kind=kLoop, calls=%fused_computation | loop fusion | flops 131072 | bytes 1050624 | tf_op jit(solution)/shard_map/mul | solution.py:236

commit v3 on v2

--- a/solution.py
+++ b/solution.py
@@ -16,8 +16,8 @@
 
 def kernel(
     sim_hbm, pat_ref, acc, scale_ref,
-    sim, left, right, p1, p2,
-    in_sem, z_send, z_recv, f_send, f_recv, s_send, s_recv, d_send, d_recv,
+    sim, left, right, p1, p2, raw, scales,
+    in_sem, z_send, z_recv, r_send, r_recv, c_send, c_recv, f_send, f_recv, s_send, s_recv, d_send, d_recv,
     p_send, p_recv,
 ):
     row = lax.axis_index("row")
@@ -52,12 +52,11 @@
         pl.semaphore_signal(barrier, inc=1, device_id=(peer, z), device_id_type=MESH)
     for peer in (z_next, z_prev):
         pl.semaphore_signal(barrier, inc=1, device_id=(row, peer), device_id_type=MESH)
-    p_left = pat_ref[0, 0].astype(jnp.float32)
-    p_right = pat_ref[0, 1].astype(jnp.float32)
+    cells = jnp.where(
+        lax.broadcasted_iota(jnp.int32, (1, sim.shape[1]), 1) < TILE, pat_ref[0, 0], pat_ref[0, 1]
+    ).astype(jnp.float32)
     load.wait()
-    sim[:, :TILE] = sim[:, :TILE] * p_left
-    sim[:, TILE:] = sim[:, TILE:] * p_right
-    part = jnp.sum(sim[...], axis=0, keepdims=True)
+    part = jnp.sum(sim[...], axis=0, keepdims=True) * cells
     pl.semaphore_wait(barrier, len(peers) + 2)
 
     pending = []
@@ -81,8 +80,20 @@
             copy.wait_recv()
         return jnp.sum(parts[...], axis=0)
 
+    ways = ((1, z_next), (-1, z_prev))
+    raw_copies = [
+        send(sim.at[pl.ds(w * HALF, HALF)], raw.at[w], r_send.at[w], r_recv.at[w], (row, peer))
+        for w, (_, peer) in enumerate(ways)
+    ]
+
     total = plane_sum(part, p1, 0)
-    operand = (sim[...] * (total_rows / total)).astype(jnp.bfloat16)
+    scale = cells * (total_rows / total)
+    scales[2] = scale
+    scale_copies = [
+        send(scales.at[2], scales.at[w], c_send.at[w], c_recv.at[w], (row, peer))
+        for w, (_, peer) in enumerate(ways)
+    ]
+    operand = (sim[...] * scale).astype(jnp.bfloat16)
     left[z] = operand
 
     def block(r):
@@ -90,6 +101,7 @@
 
     right[chip, pl.ds(core * TILE, TILE)] = operand
 
+    last = NZ - 2
     z_copies = {}
 
     def z_hop(way, j):
@@ -98,6 +110,17 @@
         ref = left.at[origin, pl.ds(half * HALF, HALF)]
         w = 0 if way > 0 else 1
         z_copies[way, j] = send(ref, ref, z_send.at[w, j], z_recv.at[w, j], (row, z_next if way > 0 else z_prev))
+
+    def z_take(way, j):
+        if j == 0:
+            w = 0 if way > 0 else 1
+            raw_copies[w].wait_recv()
+            scale_copies[w].wait_recv()
+            left[z_prev if way > 0 else z_next, pl.ds(w * HALF, HALF)] = (raw[w] * scales[w]).astype(jnp.bfloat16)
+        else:
+            z_copies[way, j].wait_recv()
+        if j + 2 <= last:
+            z_hop(way, j + 2)
 
     plane = {}
 
@@ -147,13 +170,11 @@
                 s_hop(g, 2, ds, way)
             share(F_OFF[g], ds)
 
-    z_hop(1, 0)
-    z_hop(-1, 0)
+    z_hop(1, 1)
+    z_hop(-1, 1)
     f_hop(0, 0, 1)
     f_hop(1, 0, -1)
     spread(0)
-    z_hop(1, 1)
-    z_hop(-1, 1)
     share(0, 0)
 
     def products(first, count):
@@ -166,39 +187,32 @@
     acc[...] = jnp.zeros_like(acc)
 
     after = {
-        1: [("f", 0), ("f", 1), ("s", 0, 0), ("s", 0, 1)],
-        3: [("s", 1, 1)],
-        4: [("f", 2), ("s", 0, 2), ("s", 2, 1)],
-        5: [("s", 1, 0), ("s", 1, 2)],
-        6: [("s", 3, 1), ("s", 2, 0)],
-        7: [("s", 3, 0), ("s", 3, 2)],
-        8: [("s", 2, 2)],
+        3: [("f", 0), ("f", 1), ("s", 0, 0), ("s", 0, 1)],
+        5: [("s", 1, 1)],
+        6: [("f", 2), ("s", 0, 2), ("s", 2, 1)],
+        7: [("s", 1, 0), ("s", 1, 2)],
+        8: [("s", 3, 1), ("s", 2, 0)],
+        9: [("s", 3, 0), ("s", 3, 2)],
+        10: [("s", 2, 2)],
     }
     compute = {
-        10: [(-1, 3)],
-        11: [(2, 2), (-3, 2)],
-        12: [(4, 2), (-5, 2)],
+        11: [(-2, 5)],
+        12: [(3, 3), (-5, 3)],
         13: [(6, 2), (-7, 2)],
         14: [(8, 1)],
     }
-    last = NZ - 2
     for j in range(last + 1):
-        for way in (1, -1):
-            z_copies[way, j].wait_recv()
-            if j + 2 <= last:
-                z_hop(way, j + 2)
+        z_take(1, j)
+        z_take(-1, j)
         for key in after.get(j, ()):
             arrive(key)
-        if j == 9:
+        if j == 11:
             for copy in to_sibling:
                 copy.wait_recv()
         for first, count in compute.get(j, ()):
             products(first, count)
 
-    left_part = acc[:, :TILE] * p_left
-    right_part = acc[:, TILE:] * p_right
-    acc[:, :TILE] = left_part * left_part
-    acc[:, TILE:] = right_part * right_part
+    acc[...] = jnp.square(acc[...] * cells)
     sums = plane_sum(jnp.sum(acc[...], axis=0, keepdims=True), p2, len(peers))
     scale_ref[...] = total_rows / sums
 
@@ -227,7 +241,10 @@
             pltpu.VMEM((NX * NY, 2 * rows, columns), jnp.bfloat16),
             pltpu.VMEM((planes, 1, columns), jnp.float32),
             pltpu.VMEM((planes, 1, columns), jnp.float32),
-            dma, dma((2, NZ - 1)), dma((2, NZ - 1)), dma((3,)), dma((3,)),
+            pltpu.VMEM((2, HALF, columns), jnp.float32),
+            pltpu.VMEM((3, 1, columns), jnp.float32),
+            dma, dma((2, NZ - 1)), dma((2, NZ - 1)), dma((2,)), dma((2,)), dma((2,)), dma((2,)),
+            dma((3,)), dma((3,)),
             dma((4, 3)), dma((4, 3)), dma((NX * NY,)), dma((NX * NY,)),
             dma((2 * planes - 2,)), dma((2 * planes - 2,)),
         ],

time: 74.2 us -> 72.2 us (0.973)
  Pallas kernels: 73.1 us -> 71.2 us
    pallas_call x1, Pallas kernels: 73.1 us -> 71.2 us  [shards(): pl.pallas_call(kernel, out_shape=(pltpu.VMEM((rows, columns), jnp.float32...]
where the time goes in v3:
time: 72.2 us; the launch traced here: 72.1 us
  Pallas kernels  71.2 us (99%)
  other arithmetic  0.86 us (1%)
    pallas_call x1, Pallas kernels, shards(): pl.pallas_call(kernel, out_shape=(pltpu.VMEM((rows, columns), jnp.float32...  71.2 us

profile of v3, /device:TPU:1, one launch (start us, length us, event | category | flops | bytes accessed | tf_op | source)
XLA Modules:
  0.0 72.1 jit_solution(16174825541804633135)
XLA Ops:
  0.0 71.2 %shard_map.28 = (f32[256,512]{1,0:T(8,128)S(1)}, f32[1,512]{1,0:T(1,128)S(1)}) custom-call(f32[256,512]{1,0:T(8,128)} %sim_hbm.1, s32[1,2]{1,0:T(1,128)} %pat_ref.1), custom_call_target="tpu_custom_call" | custom-call | tf_op jit(solution)/shard_map/pallas_call | solution.py:227
  71.2 0.9 %broadcast_multiply_fusion = f32[256,512]{1,0:T(8,128)} fusion(f32[256,512]{1,0:T(8,128)S(1)} %get-tuple-element.7, f32[512]{0:T(512)S(1)} %bitcast.1), kind=kLoop, calls=%fused_computation | loop fusion | flops 131072 | bytes 1050624 | tf_op jit(solution)/shard_map/mul | solution.py:253

commit v4 on v3

--- a/solution.py
+++ b/solution.py
@@ -76,6 +76,10 @@
             send(parts.at[row], parts.at[row], p_send.at[base + i], p_recv.at[base + i], (peer, z))
             for i, peer in enumerate(peers)
         ]
+        if base:
+            for copy in pending[:-len(copies)]:
+                copy.wait_send()
+            del pending[:-len(copies)]
         for copy in copies:
             copy.wait_recv()
         return jnp.sum(parts[...], axis=0)
@@ -199,12 +203,13 @@
         11: [(-2, 5)],
         12: [(3, 3), (-5, 3)],
         13: [(6, 2), (-7, 2)],
-        14: [(8, 1)],
     }
     for j in range(last + 1):
         z_take(1, j)
+        for key in after.get(j, ())[:len(after.get(j, ())) // 2]:
+            arrive(key)
         z_take(-1, j)
-        for key in after.get(j, ()):
+        for key in after.get(j, ())[len(after.get(j, ())) // 2:]:
             arrive(key)
         if j == 11:
             for copy in to_sibling:
@@ -212,8 +217,15 @@
         for first, count in compute.get(j, ()):
             products(first, count)
 
-    acc[...] = jnp.square(acc[...] * cells)
-    sums = plane_sum(jnp.sum(acc[...], axis=0, keepdims=True), p2, len(peers))
+    k = lax.rem(z + NZ // 2, NZ)
+    column_sum = jnp.zeros((1, sim.shape[1]), jnp.float32)
+    for h in range(2):
+        rows = pl.ds(h * HALF, HALF)
+        final = acc[rows] + jnp.dot(left[k, rows], right[k], preferred_element_type=jnp.float32)
+        final = jnp.square(final * cells)
+        acc[rows] = final
+        column_sum += jnp.sum(final, axis=0, keepdims=True)
+    sums = plane_sum(column_sum, p2, len(peers))
     scale_ref[...] = total_rows / sums
 
     for copy in pending:

time: 72.2 us -> 72.1 us (level)
  no operation moved by 1% of the time
where the time goes in v4:
time: 72.1 us; the launch traced here: 71.9 us
  Pallas kernels  71 us (98%)
  other arithmetic  0.86 us (1%)
    pallas_call x1, Pallas kernels, shards(): pl.pallas_call(kernel, out_shape=(pltpu.VMEM((rows, columns), jnp.float32...  71 us

profile of v4, /device:TPU:1, one launch (start us, length us, event | category | flops | bytes accessed | tf_op | source)
XLA Modules:
  0.0 71.9 jit_solution(11547518202316770998)
XLA Ops:
  0.0 71.0 %shard_map.28 = (f32[256,512]{1,0:T(8,128)S(1)}, f32[1,512]{1,0:T(1,128)S(1)}) custom-call(f32[256,512]{1,0:T(8,128)} %sim_hbm.1, s32[1,2]{1,0:T(1,128)} %pat_ref.1), custom_call_target="tpu_custom_call" | custom-call | tf_op jit(solution)/shard_map/pallas_call | solution.py:239
  71.0 0.9 %broadcast_multiply_fusion = f32[256,512]{1,0:T(8,128)} fusion(f32[256,512]{1,0:T(8,128)S(1)} %get-tuple-element.7, f32[512]{0:T(512)S(1)} %bitcast.1), kind=kLoop, calls=%fused_computation | loop fusion | flops 131072 | bytes 1050624 | tf_op jit(solution)/shard_map/mul | solution.py:265

commit v5 on v4

--- a/solution.py
+++ b/solution.py
@@ -205,11 +205,12 @@
         13: [(6, 2), (-7, 2)],
     }
     for j in range(last + 1):
+        ready = after.get(j, ())
+        z_take(-1, j)
+        for key in ready[:len(ready) // 2]:
+            arrive(key)
         z_take(1, j)
-        for key in after.get(j, ())[:len(after.get(j, ())) // 2]:
-            arrive(key)
-        z_take(-1, j)
-        for key in after.get(j, ())[len(after.get(j, ())) // 2:]:
+        for key in ready[len(ready) // 2:]:
             arrive(key)
         if j == 11:
             for copy in to_sibling:

time: 72.1 us -> 71.2 us (0.988)
  Pallas kernels: 71 us -> 70.2 us
    pallas_call x1, Pallas kernels: 71 us -> 70.2 us  [shards(): pl.pallas_call(kernel, out_shape=(pltpu.VMEM((rows, columns), jnp.float32...]
where the time goes in v5:
time: 71.2 us; the launch traced here: 71 us
  Pallas kernels  70.2 us (99%)
  other arithmetic  0.86 us (1%)
    pallas_call x1, Pallas kernels, shards(): pl.pallas_call(kernel, out_shape=(pltpu.VMEM((rows, columns), jnp.float32...  70.2 us

profile of v5, /device:TPU:1, one launch (start us, length us, event | category | flops | bytes accessed | tf_op | source)
XLA Modules:
  0.0 71.0 jit_solution(14389357840333909840)
XLA Ops:
  0.0 70.2 %shard_map.28 = (f32[256,512]{1,0:T(8,128)S(1)}, f32[1,512]{1,0:T(1,128)S(1)}) custom-call(f32[256,512]{1,0:T(8,128)} %sim_hbm.1, s32[1,2]{1,0:T(1,128)} %pat_ref.1), custom_call_target="tpu_custom_call" | custom-call | tf_op jit(solution)/shard_map/pallas_call | solution.py:240
  70.2 0.9 %broadcast_multiply_fusion = f32[256,512]{1,0:T(8,128)} fusion(f32[256,512]{1,0:T(8,128)S(1)} %get-tuple-element.7, f32[512]{0:T(512)S(1)} %bitcast.1), kind=kLoop, calls=%fused_computation | loop fusion | flops 131072 | bytes 1050624 | tf_op jit(solution)/shard_map/mul | solution.py:266

commit v6 on v5

--- a/solution.py
+++ b/solution.py
@@ -48,10 +48,10 @@
     sibling = row_of(x, y, 1 - core)
 
     barrier = pltpu.get_barrier_semaphore()
+    for peer in (z_next, z_prev):
+        pl.semaphore_signal(barrier, inc=1, device_id=(row, peer), device_id_type=MESH)
     for peer in peers:
         pl.semaphore_signal(barrier, inc=1, device_id=(peer, z), device_id_type=MESH)
-    for peer in (z_next, z_prev):
-        pl.semaphore_signal(barrier, inc=1, device_id=(row, peer), device_id_type=MESH)
     cells = jnp.where(
         lax.broadcasted_iota(jnp.int32, (1, sim.shape[1]), 1) < TILE, pat_ref[0, 0], pat_ref[0, 1]
     ).astype(jnp.float32)
@@ -71,9 +71,10 @@
         return copy
 
     def plane_sum(value, parts, base):
-        parts[row] = value
+        mine = parts.at[pl.ds(row, 1)]
+        mine[...] = value
         copies = [
-            send(parts.at[row], parts.at[row], p_send.at[base + i], p_recv.at[base + i], (peer, z))
+            send(mine, mine, p_send.at[base + i], p_recv.at[base + i], (peer, z))
             for i, peer in enumerate(peers)
         ]
         if base:
@@ -82,7 +83,7 @@
             del pending[:-len(copies)]
         for copy in copies:
             copy.wait_recv()
-        return jnp.sum(parts[...], axis=0)
+        return jnp.sum(parts[...], axis=0, keepdims=True)
 
     ways = ((1, z_next), (-1, z_prev))
     raw_copies = [
@@ -252,8 +253,8 @@
             pltpu.VMEM((rows, columns), jnp.float32),
             pltpu.VMEM((NZ, rows, columns), jnp.bfloat16),
             pltpu.VMEM((NX * NY, 2 * rows, columns), jnp.bfloat16),
-            pltpu.VMEM((planes, 1, columns), jnp.float32),
-            pltpu.VMEM((planes, 1, columns), jnp.float32),
+            pltpu.VMEM((planes, columns), jnp.float32),
+            pltpu.VMEM((planes, columns), jnp.float32),
             pltpu.VMEM((2, HALF, columns), jnp.float32),
             pltpu.VMEM((3, 1, columns), jnp.float32),
             dma, dma((2, NZ - 1)), dma((2, NZ - 1)), dma((2,)), dma((2,)), dma((2,)), dma((2,)),

time: 71.2 us -> 71.1 us (level)
  no operation moved by 1% of the time
where the time goes in v6:
time: 71.1 us; the launch traced here: 70.9 us
  Pallas kernels  70.1 us (99%)
  other arithmetic  0.86 us (1%)
    pallas_call x1, Pallas kernels, shards(): pl.pallas_call(kernel, out_shape=(pltpu.VMEM((rows, columns), jnp.float32...  70.1 us

profile of v6, /device:TPU:1, one launch (start us, length us, event | category | flops | bytes accessed | tf_op | source)
XLA Modules:
  0.0 70.9 jit_solution(8591861702488650288)
XLA Ops:
  0.0 70.1 %shard_map.28 = (f32[256,512]{1,0:T(8,128)S(1)}, f32[1,512]{1,0:T(1,128)S(1)}) custom-call(f32[256,512]{1,0:T(8,128)} %sim_hbm.1, s32[1,2]{1,0:T(1,128)} %pat_ref.1), custom_call_target="tpu_custom_call" | custom-call | tf_op jit(solution)/shard_map/pallas_call | solution.py:241
  70.1 0.9 %broadcast_multiply_fusion = f32[256,512]{1,0:T(8,128)} fusion(f32[256,512]{1,0:T(8,128)S(1)} %get-tuple-element.7, f32[512]{0:T(512)S(1)} %bitcast.1), kind=kLoop, calls=%fused_computation | loop fusion | flops 131072 | bytes 1050624 | tf_op jit(solution)/shard_map/mul | solution.py:267
